TPU v7x, 32 devices: a whole 2x2x4 slice. The times are simulated.
32 devices in a mesh: lat: 8 (over z, y), lev: 4 (over x, core).
Axes of the slice: x: 2, y: 2, z: 4, core: 2. Of those that a mesh axis runs over, the one named last changes fastest.
Arguments:
- field: float32 [4, 320, 4096], P(None, 'lat', 'lev'), may hold values from -6 to 6
- weights: bfloat16 [4, 320, 4096], P(None, 'lat', 'lev'), may hold values from 0 to 0.5
- depart_row: int32 [320, 4096], P('lat', 'lev'), may hold values from -2 to 1
- depart_col: int32 [320, 4096], P('lat', 'lev'), may hold values from -2 to 1
- legendre: bfloat16 [320, 16, 640], P('lat'), may hold values from -6 to 6
- wave_slot: int32 [16], replicated, may hold values from 0 to 15, each once
Outputs:
- updated: float32 [4, 320, 4096], P(None, 'lat', 'lev')
- spectral: float32 [16, 2, 4, 2, 640], P('lat', None, 'lev')
Inputs may be any that keep to these rules, and one draw needn't show every extreme that they name: `depart_row`: latitude offsets of departure cells, so that rows i - 2 to i + 2 are read. `depart_col`: longitude offsets of departure cells, so that columns j - 2 to j + 2 are read, periodically. `wave_slot`: A permutation of 0 to 15.
All inputs are finite; a program needn't handle non-finite values.
Results may differ from a plain program's by a relative error of at most 0.0033.
Values may be sent and summed in bfloat16 or wider, within the bound.
A program may use at most 128 MiB of HBM per device.

v0:
```python
import math
import jax
import jax.numpy as jnp
from jax import lax
from jax.sharding import PartitionSpec as P

NLON = 4096
NT = 1279
M_OWN = 2
DAMPING = 4.0


def padded(array, sides, width, wrap):
    for axis, dim in sides:
        size, length = (lax.axis_size(axis), array.shape[dim])
        up = [(i, (i + 1) % size) for i in range(size if wrap else size - 1)]
        down = [(j, i) for i, j in up]
        last = lax.slice_in_dim(array, length - width, length, axis=dim)
        initial = lax.slice_in_dim(array, 0, width, axis=dim)
        before = lax.ppermute(last, axis, up)
        after = lax.ppermute(initial, axis, down)
        array = jnp.concatenate([before, array, after], axis=dim)
    return array


def swapped(value, axis, apart):
    mask = 2**apart
    pairs = [(source, source ^ mask) for source in range(lax.axis_size(axis))]
    return lax.ppermute(value, axis, pairs)


def forward_table(lon_list, wave_list):
    phases = lon_list[:, None] * wave_list[None, :] % NLON
    angles = phases.astype(jnp.float32) * (2.0 * math.pi / NLON)
    return jnp.concatenate([jnp.cos(angles), -jnp.sin(angles)], axis=1) * (1.0 / math.sqrt(NLON))


def inverse_table(wave_list, lon_list, wave_count):
    phases = wave_list[:, None] * lon_list[None, :] % NLON
    angles = phases.astype(jnp.float32) * (2.0 * math.pi / NLON)
    weight = (jnp.where(wave_list == 0, 1.0, 2.0) / math.sqrt(wave_count))[:, None]
    return jnp.concatenate([weight * jnp.cos(angles), -weight * jnp.sin(angles)], axis=0)


def diffuse(raw_sums, slot_waves, steps_count):
    degree = (
        slot_waves[:, None, None]
        + 2 * jnp.arange(steps_count, dtype=jnp.int32)[None, None, :]
        + jnp.arange(2, dtype=jnp.int32)[None, :, None]
    )
    inside = degree <= NT
    factor = 1.0 / (
        1.0 + DAMPING * (degree * (degree + 1)).astype(jnp.float32) / float(NT * (NT + 1))
    )
    masked = jnp.where(inside[:, :, None, None, :], raw_sums, jnp.zeros_like(raw_sums))
    damped = masked * factor[:, :, None, None, :]
    return (damped, (damped - masked).astype(jnp.bfloat16))


def on_device(field, weights, depart_row, depart_col, legendre, wave_slot):
    hp = lax.Precision.HIGHEST
    lat_count = lax.axis_size("lat")
    lev_count = lax.axis_size("lev")
    lat_here = lax.axis_index("lat")
    levels, rows_here, lon_width = field.shape
    lev_local = levels // lev_count
    wave_count = M_OWN * lat_count
    steps_count = legendre.shape[2]
    half_lat = rows_here * lat_count // 2
    northern = lat_here < lat_count // 2
    bit_count = lat_count.bit_length() - 1
    band = padded(field, (("lat", 1),), 2, False)
    padded_block = padded(band, (("lev", 2),), 2, True)
    wide_cols = lon_width + 4
    flattened = padded_block.reshape(levels, (rows_here + 4) * wide_cols)
    row_base = jnp.arange(rows_here, dtype=jnp.int32)[:, None] + 2 + depart_row
    col_base = jnp.arange(lon_width, dtype=jnp.int32)[None, :] + 2 + depart_col
    summed = jnp.zeros((levels, rows_here * lon_width), jnp.float32)
    for row_step in range(2):
        for col_step in range(2):
            source = ((row_base + row_step) * wide_cols + col_base + col_step).reshape(-1)
            corner = weights[2 * row_step + col_step].reshape(-1).astype(jnp.float32)
            summed = summed + corner[None, :] * jnp.take(flattened, source, axis=1)
    advected = summed.reshape(levels, rows_here, lon_width)
    wavenumbers = jnp.arange(wave_count, dtype=jnp.int32) * (NT + 1) // wave_count
    one_hot = (wave_slot[None, :] == jnp.arange(wave_count, dtype=jnp.int32)[:, None]).astype(
        jnp.int32
    )
    k_of_slot = jnp.sum(one_hot * jnp.arange(wave_count, dtype=jnp.int32)[None, :], axis=1)
    slot_waves = jnp.sum(one_hot * wavenumbers[None, :], axis=1)
    columns = lax.all_to_all(advected, "lev", split_axis=0, concat_axis=2, tiled=True)
    wave_table = forward_table(jnp.arange(NLON, dtype=jnp.int32), wavenumbers)
    coeffs = jnp.dot(
        columns.reshape(-1, NLON), wave_table, precision=hp, preferred_element_type=jnp.float32
    )
    fourier = coeffs.reshape(lev_local, rows_here, 2, wave_count).astype(jnp.bfloat16)
    partner = fourier
    for bit_number in range(bit_count):
        partner = swapped(partner, "lat", bit_number)
    partner = jnp.flip(partner, axis=1)
    forward_scale = 1.0 / math.sqrt(half_lat)
    parity = jnp.where(northern, 0, 1).astype(jnp.int32)
    inverse_scale = 1.0 / math.sqrt(steps_count)
    chosen = k_of_slot
    leg_part = jnp.take(legendre, chosen, axis=1)
    own_part = jnp.take(fourier, chosen, axis=3)
    other_part = jnp.take(partner, chosen, axis=3)
    own_term = jnp.einsum("lkj,vlck->kvcj", leg_part, own_part, preferred_element_type=jnp.float32)
    other_term = jnp.einsum(
        "lkj,vlck->kvcj", leg_part, other_part, preferred_element_type=jnp.float32
    )
    combined = jnp.where(northern, own_term + other_term, other_term - own_term) * forward_scale
    nothing = jnp.zeros_like(combined)
    owned_sums = lax.psum_scatter(
        jnp.stack(
            [jnp.where(northern, combined, nothing), jnp.where(northern, nothing, combined)], axis=1
        ),
        "lat",
        scatter_dimension=0,
        tiled=True,
    )
    own_waves = lax.dynamic_slice_in_dim(slot_waves, lat_here * M_OWN, M_OWN, 0)
    damped, change = diffuse(owned_sums, own_waves, steps_count)
    chosen = k_of_slot
    leg_part = jnp.take(legendre, chosen, axis=1)
    own_parity = lax.dynamic_index_in_dim(
        lax.all_gather(change, "lat", axis=0, tiled=True), parity, 1, keepdims=False
    )
    result = jnp.einsum("lkj,kvcj->vlck", leg_part, own_parity, preferred_element_type=jnp.float32)
    half_sum = result * inverse_scale
    across = half_sum
    for bit_number in range(bit_count):
        across = swapped(across, "lat", bit_number)
    across = jnp.flip(across, axis=1)
    synthesis = jnp.where(northern, half_sum + across, across - half_sum)
    synthesis = synthesis.reshape(lev_local, rows_here, 2 * wave_count)
    back_table = inverse_table(slot_waves, jnp.arange(NLON, dtype=jnp.int32), wave_count)
    circles = jnp.dot(
        synthesis.reshape(-1, 2 * wave_count),
        back_table,
        precision=hp,
        preferred_element_type=jnp.float32,
    ).reshape(lev_local, rows_here, NLON)
    increment = lax.all_to_all(circles, "lev", split_axis=2, concat_axis=0, tiled=True)
    updated = advected + increment
    return (updated, damped)


def solution(mesh):
    placed = (
        P(None, "lat", "lev"),
        P(None, "lat", "lev"),
        P("lat", "lev"),
        P("lat", "lev"),
        P("lat", None, None),
        P(),
    )
    return jax.shard_map(
        on_device,
        mesh=mesh,
        in_specs=placed,
        out_specs=(P(None, "lat", "lev"), P("lat", None, "lev", None, None)),
        check_vma=False,
    )
```

profile of v0, /device:TPU:0, one launch (start us, length us, event | category | flops | bytes accessed | tf_op | source)
XLA Modules:
  0.0 875.8 jit_solution(8156510227616605305)
XLA Ops:
  7.2 1.1 fusion.52
  8.3 4.9 collective-permute-start
  13.2 1.3 collective-permute-start.1
  14.5 1.1 fusion.43
  18.8 1.1 convert_bitcast_fusion.3
  19.8 1.9 fusion.29
  21.8 1.3 select_reduce_fusion.1
  23.6 1.2 pad_maximum_fusion
  25.5 1.7 collective-permute-start.3
  30.1 3.0 gather_fusion.5
  33.7 1.4 concatenate.13
  35.9 11.3 %copy.81 = f32[4,45232]{0,1:T(8,128)} copy(f32[4,45232]{1,0:T(4,128)S(1)} %reshape.196) | data formatting | bytes 1447424 | tf_op jit(solution)/shard_map/reshape | solution.py:75
  47.2 142.5 %gather_fusion = f32[40960,4]{1,0:T(8,128)} fusion(f32[4,45232]{0,1:T(8,128)} %copy.81, s32[40960]{0:T(1024)S(1)} %copy-done.4), kind=kCustom, calls=%fused_computation.clone | custom fusion | bytes 1474560 | tf_op jit(solution)/shard_map/jit(_take)/gather | solution.py:83
  189.7 11.4 %copy.82 = f32[40960,4]{0,1:T(4,128)S(1)} copy(f32[40960,4]{1,0:T(8,128)} %gather_fusion) | data formatting | bytes 1310720 | tf_op jit(solution)/shard_map/jit(_take)/gather | solution.py:83
  201.1 142.5 %gather_fusion.1 = f32[40960,4]{1,0:T(8,128)} fusion(f32[4,45232]{0,1:T(8,128)} %copy.81, s32[40960]{0:T(1024)S(1)} %copy-done.5), kind=kCustom, calls=%fused_computation.3.clone | custom fusion | bytes 1474560 | tf_op jit(solution)/shard_map/jit(_take)/gather | solution.py:83
  343.6 11.4 %copy.84 = f32[40960,4]{0,1:T(4,128)S(1)} copy(f32[40960,4]{1,0:T(8,128)} %gather_fusion.1) | data formatting | bytes 1310720 | tf_op jit(solution)/shard_map/jit(_take)/gather | solution.py:83
  355.1 142.5 %gather_fusion.2 = f32[40960,4]{1,0:T(8,128)} fusion(f32[4,45232]{0,1:T(8,128)} %copy.81, s32[40960]{0:T(1024)S(1)} %copy-done.3), kind=kCustom, calls=%fused_computation.4.clone | custom fusion | bytes 1474560 | tf_op jit(solution)/shard_map/jit(_take)/gather | solution.py:83
  497.6 12.2 %copy.86 = f32[40960,4]{0,1:T(4,128)} copy(f32[40960,4]{1,0:T(8,128)} %gather_fusion.2) | data formatting | bytes 1310720 | tf_op jit(solution)/shard_map/jit(_take)/gather | solution.py:83
  509.7 142.5 %gather_fusion.3 = f32[40960,4]{1,0:T(8,128)} fusion(f32[4,45232]{0,1:T(8,128)} %copy.81, s32[40960]{0:T(1024)S(1)} %fusion.28), kind=kCustom, calls=%fused_computation.5.clone | custom fusion | bytes 1474560 | tf_op jit(solution)/shard_map/jit(_take)/gather | solution.py:83
  652.3 12.2 %copy.88 = f32[40960,4]{0,1:T(4,128)} copy(f32[40960,4]{1,0:T(8,128)} %gather_fusion.3) | data formatting | bytes 1310720 | tf_op jit(solution)/shard_map/jit(_take)/gather | solution.py:83
  664.5 2.4 fusion.1
  667.7 1.2 copy.124
  668.9 3.5 all-to-all-start
  672.8 1.1 maximum_multiply_fusion
  673.9 8.7 all-to-all-done
  684.1 2.7 collective-permute-start.4
  688.5 3.0 collective-permute-start.5
  691.5 1.6 collective-permute-done.5
  693.1 3.0 collective-permute-start.6
  696.1 1.3 dynamic-slice
  699.7 0.9 fusion.5
  700.7 0.9 select_bitcast_fusion.2
  702.4 68.8 %all-reduce.3.cloned.1.call-done = f32[16,2,1,2,640]{4,3,0,2,1:T(2,128)} async-done(((f32[16,2,1,2,640]{4,3,0,2,1:T(2,128)}), f32[16,2,1,2,640]{4,3,0,2,1:T(2,128)}) %all-reduce.3.cloned.1.call-update) | async-done | bytes 163856
  771.9 30.6 %all_gather.3 = bf16[16,2,1,2,640]{4,3,0,2,1:T(2,128)(2,1)S(1)} all-gather(bf16[2,2,1,2,640]{4,3,0,2,1:T(2,128)(2,1)S(1)} %get-tuple-element.19), channel_id=1, replica_groups=mesh['lat'=8,'lev'=4] {'lat'}, dimensions={0}, use_global_device_ids=true | all-gather | bytes 92160 | tf_op jit(solution)/shard_map/all_gather | solution.py:127
  803.3 3.3 collective-permute-done.7
  807.3 3.1 collective-permute-done.8
  810.6 1.7 cosine_multiply_fusion
  812.3 2.7 collective-permute-done.9
  815.2 3.4 fusion.9
  819.2 19.4 %reduce = f32[4096,40]{1,0:T(8,128)} reduce(f32[4096,1,40]{2,1,0:T(1,128)S(1)} %bitcast.113, f32[]{:T(128)} %broadcast.351), dimensions={1}, to_apply=%bitcast.100.reduce_sub_computation | reduce | bytes 1310724
  838.6 3.9 reshape.301
  842.5 3.7 all-to-all-start.1
  846.9 9.4 %all-to-all-done.1 = f32[4,1,40960]{2,1,0:T(1,128)S(1)} async-done(((f32[4,1,40960]{2,1,0:T(1,128)}), f32[4,1,40960]{2,1,0:T(1,128)S(1)}, u32[]{:S(2)}, u32[]{:S(2)}) %all-to-all-start.1) | async-done | bytes 655392 | tf_op jit(solution)/shard_map/all_to_all | solution.py:144
  856.2 3.4 reduce.1
  859.6 5.1 reshape.302
  864.7 1.6 copy.101
  866.3 1.5 bitcast_add_fusion
  867.7 1.2 copy.99
  (79 shorter events, 19.0 us)
Async XLA Ops:
  7.2 22.9 %copy-start = (bf16[40,16,640]{2,1,0:T(8,128)(2,1)S(1)}, bf16[40,16,640]{2,1,0:T(8,128)(2,1)}, u32[]{:S(2)}) copy-start(bf16[40,16,640]{2,1,0:T(8,128)(2,1)} %param.16) | copy-start | bytes 2457604
  8.3 15.3 %collective-permute-start = (f32[4,2,1024]{2,1,0:T(2,128)S(1)}, f32[4,2,1024]{2,1,0:T(2,128)S(1)}, u32[]{:S(2)}, u32[]{:S(2)}) collective-permute-start(f32[4,2,1024]{2,1,0:T(2,128)S(1)} %get-tuple-element.23), channel_id=1, source_target_pairs={{0,4},{4,8},{8,12},{12,16},{16,20},{20,24},{24,28},{1,5},{5,9},{9,... | collective-permute-start | bytes 98312 | tf_op jit(solution)/shard_map/ppermute | solution.py:20
  13.2 10.4 %collective-permute-start.1 = (f32[4,2,1024]{2,1,0:T(2,128)S(1)}, f32[4,2,1024]{2,1,0:T(2,128)S(1)}, u32[]{:S(2)}, u32[]{:S(2)}) collective-permute-start(f32[4,2,1024]{2,1,0:T(2,128)S(1)} %get-tuple-element.24), channel_id=1, source_target_pairs={{4,0},{8,4},{12,8},{16,12},{20,16},{24,20},{28,24},{5,1},{9,5},{13... | collective-permute-start | bytes 98312 | tf_op jit(solution)/shard_map/ppermute | solution.py:21
  25.5 7.5 collective-permute-start.2
  25.5 8.2 collective-permute-start.3
  27.3 5.8 copy-start.9
  33.0 14.1 %copy-start.4 = (s32[40960]{0:T(1024)S(1)}, s32[40960]{0:T(1024)}, u32[]{:S(2)}) copy-start(s32[40960]{0:T(1024)} %fusion.25) | copy-start | bytes 491524
  33.1 0.7 copy-start.8
  35.9 165.2 %copy-start.5 = (s32[40960]{0:T(1024)S(1)}, s32[40960]{0:T(1024)}, u32[]{:S(2)}) copy-start(s32[40960]{0:T(1024)} %fusion.26) | copy-start | bytes 491524
  189.7 165.4 %copy-start.3 = (s32[40960]{0:T(1024)S(1)}, s32[40960]{0:T(1024)}, u32[]{:S(2)}) copy-start(s32[40960]{0:T(1024)} %fusion.27) | copy-start | bytes 491524
  497.6 166.9 %copy-start.6 = (f32[5,8,8,128]{3,1,2,0:T(8,128)S(1)}, f32[5,8,8,128]{3,1,2,0:T(8,128)}, u32[]{:S(2)}) copy-start(f32[5,8,8,128]{3,1,2,0:T(8,128)} %copy.104) | copy-start | bytes 491524
  497.6 166.9 %copy-start.7 = (f32[5,8,8,128]{3,1,2,0:T(8,128)S(1)}, f32[5,8,8,128]{3,1,2,0:T(8,128)}, u32[]{:S(2)}) copy-start(f32[5,8,8,128]{3,1,2,0:T(8,128)} %copy.106) | copy-start | bytes 491524
  509.7 162.9 %copy-start.10 = (pred[16]{0:T(512)(128)(4,1)S(1)}, pred[16]{0:T(512)(128)(4,1)}, u32[]{:S(2)}) copy-start(pred[16]{0:T(512)(128)(4,1)} %compare_and_fusion.4) | copy-start | bytes 52
  652.2 216.7 %copy-start.1 = (bf16[40,16,640]{2,1,0:T(8,128)(2,1)S(1)}, bf16[40,16,640]{2,1,0:T(8,128)(2,1)}, u32[]{:S(2)}) copy-start(bf16[40,16,640]{2,1,0:T(8,128)(2,1)} %param.16) | copy-start | bytes 2457604
  666.8 0.8 copy-start.2
  668.9 13.7 %all-to-all-start = ((f32[4,40,1024]{2,1,0:T(8,128)}), f32[4,40,1024]{2,1,0:T(8,128)S(1)}, u32[]{:S(2)}, u32[]{:S(2)}) async-start(f32[4,40,1024]{2,1,0:T(8,128)} %bitcast.109), calls=%async_computation | async-start | bytes 1310720 | tf_op jit(solution)/shard_map/all_to_all | solution.py:91
  672.4 98.8 %all-reduce.3.cloned.1.call-start = ((), (), s32[]{:S(2)}) async-start(), calls=%async_computation.2 | async-start | bytes 327680
  684.1 4.3 collective-permute-start.4
  688.5 4.6 collective-permute-start.5
  693.1 5.8 collective-permute-start.6
  802.9 3.8 collective-permute-start.7
  806.6 3.7 collective-permute-start.8
  810.4 4.6 collective-permute-start.9
  842.5 13.7 %all-to-all-start.1 = ((f32[4,1,40960]{2,1,0:T(1,128)}), f32[4,1,40960]{2,1,0:T(1,128)S(1)}, u32[]{:S(2)}, u32[]{:S(2)}) async-start(f32[4,1,40960]{2,1,0:T(1,128)} %reshape.301), calls=%async_computation.1 | async-start | bytes 1310720 | tf_op jit(solution)/shard_map/all_to_all | solution.py:144
Sparse Core Ops, SparseCore 0:
  702.5 68.6 all-reduce.2
where the time goes:
time: 877 us; the launch traced here: 876 us
  local copies, waits for them, and re-layouts  659 us (75%)
  waiting for transfers between devices  98.5 us (11%)
  other arithmetic  42 us (5%)
  blocking collectives  30.6 us (3%)
  starting transfers between devices  24.7 us (3%)
  between operations  15.1 us (2%)
    gather x8, local copies, waits for them, and re-layouts, on_device(): summed = summed + corner[None, :] * jnp.take(flattened, source, axis=1)  617 us
    unnamed x2, waiting for transfers between devices  68.8 us
    all_gather x1, blocking collectives, on_device(): lax.all_gather(change, 'lat', axis=0, tiled=True)  30.6 us
    unnamed x3, other arithmetic  21.6 us
    unnamed x37, local copies, waits for them, and re-layouts  18.4 us
  transfers between devices with their start and end apart: 13, of which 8 were waited for; matrix products, arithmetic and copies ran while one was open for 2% of the time, Pallas kernels for 0%

commit v1 on v0

--- a/solution.py
+++ b/solution.py
@@ -141,7 +141,15 @@
         precision=hp,
         preferred_element_type=jnp.float32,
     ).reshape(lev_local, rows_here, NLON)
-    increment = lax.all_to_all(circles, "lev", split_axis=2, concat_axis=0, tiled=True)
+    increment = jnp.concatenate(
+        lax.all_to_all(
+            jnp.stack(jnp.split(circles, lax.psum(1, axis_name="lev"), 2), axis=0),
+            axis_name="lev",
+            split_axis=0,
+            concat_axis=0,
+        ),
+        0,
+    )
     updated = advected + increment
     return (updated, damped)
 

time: 877 us -> 845 us (0.964)
  other arithmetic: 42 us -> 20 us
  local copies, waits for them, and re-layouts: 659 us -> 650 us
    unnamed x3 -> x2, other arithmetic: 21.6 us -> 2.18 us
    unnamed x37 -> x31, local copies, waits for them, and re-layouts: 18.4 us -> 6.64 us
  transfers between devices with their start and end apart: 13 -> 13, of which waited for: 8 -> 8; matrix products, arithmetic and copies ran while one was open for 2% -> 3% of each run, Pallas kernels for 0% -> 0%
where the time goes in v1:
time: 845 us; the launch traced here: 843 us
  local copies, waits for them, and re-layouts  650 us (77%)
  waiting for transfers between devices  99 us (12%)
  blocking collectives  30.6 us (4%)
  starting transfers between devices  25.2 us (3%)
  other arithmetic  20 us (2%)
  between operations  15 us (2%)
    gather x8, local copies, waits for them, and re-layouts, on_device(): summed = summed + corner[None, :] * jnp.take(flattened, source, axis=1)  619 us
    unnamed x2, waiting for transfers between devices  68.9 us
    all_gather x1, blocking collectives, on_device(): lax.all_gather(change, 'lat', axis=0, tiled=True)  30.6 us
  transfers between devices with their start and end apart: 13, of which 8 were waited for; matrix products, arithmetic and copies ran while one was open for 3% of the time, Pallas kernels for 0%

profile of v1, /device:TPU:0, one launch (start us, length us, event | category | flops | bytes accessed | tf_op | source)
XLA Modules:
  0.0 843.5 jit_solution(8111631968260475637)
XLA Ops:
  7.2 1.1 fusion.51
  8.3 4.9 collective-permute-start
  13.2 1.3 collective-permute-start.1
  14.5 1.1 fusion.42
  18.8 1.1 convert_bitcast_fusion.3
  19.8 1.9 fusion.28
  21.8 1.3 select_reduce_fusion.1
  23.6 1.2 pad_maximum_fusion
  25.5 1.7 collective-permute-start.3
  30.1 3.0 gather_fusion.5
  33.7 1.4 concatenate.13
  35.1 0.8 reshape.199
  35.9 11.2 %copy.56 = f32[4,45232]{0,1:T(8,128)} copy(f32[4,45232]{1,0:T(4,128)S(1)} %reshape.199) | data formatting | bytes 1447424 | tf_op jit(solution)/shard_map/reshape | solution.py:75
  47.2 142.8 %gather_fusion = f32[40960,4]{1,0:T(8,128)} fusion(f32[4,45232]{0,1:T(8,128)} %copy.56, s32[40960]{0:T(1024)S(1)} %copy-done.3), kind=kCustom, calls=%fused_computation.clone | custom fusion | bytes 1474560 | tf_op jit(solution)/shard_map/jit(_take)/gather | solution.py:83
  189.9 11.4 %copy.57 = f32[40960,4]{0,1:T(4,128)S(1)} copy(f32[40960,4]{1,0:T(8,128)} %gather_fusion) | data formatting | bytes 1310720 | tf_op jit(solution)/shard_map/jit(_take)/gather | solution.py:83
  201.4 142.8 %gather_fusion.1 = f32[40960,4]{1,0:T(8,128)} fusion(f32[4,45232]{0,1:T(8,128)} %copy.56, s32[40960]{0:T(1024)S(1)} %copy-done.4), kind=kCustom, calls=%fused_computation.3.clone | custom fusion | bytes 1474560 | tf_op jit(solution)/shard_map/jit(_take)/gather | solution.py:83
  344.2 12.1 %copy.59 = f32[40960,4]{0,1:T(4,128)} copy(f32[40960,4]{1,0:T(8,128)} %gather_fusion.1) | data formatting | bytes 1310720 | tf_op jit(solution)/shard_map/jit(_take)/gather | solution.py:83
  356.3 142.8 %gather_fusion.2 = f32[40960,4]{1,0:T(8,128)} fusion(f32[4,45232]{0,1:T(8,128)} %copy.56, s32[40960]{0:T(1024)S(1)} %copy-done.2), kind=kCustom, calls=%fused_computation.4.clone | custom fusion | bytes 1474560 | tf_op jit(solution)/shard_map/jit(_take)/gather | solution.py:83
  499.0 12.2 %copy.61 = f32[40960,4]{0,1:T(4,128)} copy(f32[40960,4]{1,0:T(8,128)} %gather_fusion.2) | data formatting | bytes 1310720 | tf_op jit(solution)/shard_map/jit(_take)/gather | solution.py:83
  511.2 142.8 %gather_fusion.3 = f32[40960,4]{1,0:T(8,128)} fusion(f32[4,45232]{0,1:T(8,128)} %copy.56, s32[40960]{0:T(1024)S(1)} %fusion.27), kind=kCustom, calls=%fused_computation.5.clone | custom fusion | bytes 1474560 | tf_op jit(solution)/shard_map/jit(_take)/gather | solution.py:83
  654.1 12.1 %copy.63 = f32[40960,4]{0,1:T(4,128)} copy(f32[40960,4]{1,0:T(8,128)} %gather_fusion.3) | data formatting | bytes 1310720 | tf_op jit(solution)/shard_map/jit(_take)/gather | solution.py:83
  666.2 2.6 fusion.1
  668.8 1.2 copy.96
  670.0 4.2 all-to-all-start
  674.6 1.1 maximum_multiply_fusion
  675.7 8.8 %all-to-all-done = f32[4,40,1024]{2,1,0:T(8,128)} async-done(((f32[4,40,1024]{2,1,0:T(8,128)}), f32[4,40,1024]{2,1,0:T(8,128)}, u32[]{:S(2)}, u32[]{:S(2)}) %all-to-all-start) | async-done | bytes 655392 | tf_op jit(solution)/shard_map/all_to_all | solution.py:91
  684.5 2.3 copy.64
  686.8 1.5 reshape.300
  689.0 2.7 collective-permute-start.4
  692.4 1.0 collective-permute-done.4
  693.3 3.0 collective-permute-start.5
  696.4 1.6 collective-permute-done.5
  697.9 3.0 collective-permute-start.6
  701.0 1.2 dynamic-slice
  704.5 1.0 fusion.5
  705.4 1.0 select_bitcast_fusion.2
  706.4 0.7 pad_maximum_fusion.2
  707.2 68.8 %all-reduce.3.cloned.1.call-done = f32[16,2,1,2,640]{4,3,0,2,1:T(2,128)} async-done(((f32[16,2,1,2,640]{4,3,0,2,1:T(2,128)}), f32[16,2,1,2,640]{4,3,0,2,1:T(2,128)}) %all-reduce.3.cloned.1.call-update) | async-done | bytes 163856
  776.0 0.8 subtract_convert_fusion
  776.8 30.6 %all_gather.3 = bf16[16,2,1,2,640]{4,3,0,2,1:T(2,128)(2,1)S(1)} all-gather(bf16[2,2,1,2,640]{4,3,0,2,1:T(2,128)(2,1)S(1)} %get-tuple-element.17), channel_id=1, replica_groups=mesh['lat'=8,'lev'=4] {'lat'}, dimensions={0}, use_global_device_ids=true | all-gather | bytes 92160 | tf_op jit(solution)/shard_map/all_gather | solution.py:127
  808.2 3.3 collective-permute-done.7
  812.1 3.1 collective-permute-done.8
  815.4 1.7 cosine_multiply_fusion
  817.2 2.7 collective-permute-done.9
  820.8 0.9 pad_maximum_fusion.1
  821.7 3.5 all-to-all-start.1
  825.8 9.6 %all-to-all-done.1 = f32[4,1,40,1024]{3,2,1,0:T(8,128)S(1)} async-done(((f32[4,1,40,1024]{3,2,1,0:T(8,128)}), f32[4,1,40,1024]{3,2,1,0:T(8,128)S(1)}, u32[]{:S(2)}, u32[]{:S(2)}) %all-to-all-start.1) | async-done | bytes 655392 | tf_op jit(solution)/shard_map/all_to_all | solution.py:145
  835.4 1.2 bitcast_add_fusion
  (72 shorter events, 14.3 us)
Async XLA Ops:
  7.2 22.9 %copy-start = (bf16[40,16,640]{2,1,0:T(8,128)(2,1)S(1)}, bf16[40,16,640]{2,1,0:T(8,128)(2,1)}, u32[]{:S(2)}) copy-start(bf16[40,16,640]{2,1,0:T(8,128)(2,1)} %param.16) | copy-start | bytes 2457604
  8.3 15.4 %collective-permute-start = (f32[4,2,1024]{2,1,0:T(2,128)S(1)}, f32[4,2,1024]{2,1,0:T(2,128)S(1)}, u32[]{:S(2)}, u32[]{:S(2)}) collective-permute-start(f32[4,2,1024]{2,1,0:T(2,128)S(1)} %get-tuple-element.25), channel_id=1, source_target_pairs={{0,4},{4,8},{8,12},{12,16},{16,20},{20,24},{24,28},{1,5},{5,9},{9,... | collective-permute-start | bytes 98312 | tf_op jit(solution)/shard_map/ppermute | solution.py:20
  13.2 10.5 %collective-permute-start.1 = (f32[4,2,1024]{2,1,0:T(2,128)S(1)}, f32[4,2,1024]{2,1,0:T(2,128)S(1)}, u32[]{:S(2)}, u32[]{:S(2)}) collective-permute-start(f32[4,2,1024]{2,1,0:T(2,128)S(1)} %get-tuple-element.26), channel_id=1, source_target_pairs={{4,0},{8,4},{12,8},{16,12},{20,16},{24,20},{28,24},{5,1},{9,5},{13... | collective-permute-start | bytes 98312 | tf_op jit(solution)/shard_map/ppermute | solution.py:21
  25.5 7.5 collective-permute-start.2
  25.5 8.2 collective-permute-start.3
  27.3 5.8 copy-start.8
  33.0 14.1 %copy-start.3 = (s32[40960]{0:T(1024)S(1)}, s32[40960]{0:T(1024)}, u32[]{:S(2)}) copy-start(s32[40960]{0:T(1024)} %fusion.24) | copy-start | bytes 491524
  33.1 0.6 copy-start.7
  35.9 165.5 %copy-start.4 = (s32[40960]{0:T(1024)S(1)}, s32[40960]{0:T(1024)}, u32[]{:S(2)}) copy-start(s32[40960]{0:T(1024)} %fusion.25) | copy-start | bytes 491524
  189.9 166.3 %copy-start.2 = (s32[40960]{0:T(1024)S(1)}, s32[40960]{0:T(1024)}, u32[]{:S(2)}) copy-start(s32[40960]{0:T(1024)} %fusion.26) | copy-start | bytes 491524
  499.0 167.1 %copy-start.5 = (f32[5,8,8,128]{3,1,2,0:T(8,128)S(1)}, f32[5,8,8,128]{3,1,2,0:T(8,128)}, u32[]{:S(2)}) copy-start(f32[5,8,8,128]{3,1,2,0:T(8,128)} %copy.74) | copy-start | bytes 491524
  499.0 167.1 %copy-start.6 = (f32[5,8,8,128]{3,1,2,0:T(8,128)S(1)}, f32[5,8,8,128]{3,1,2,0:T(8,128)}, u32[]{:S(2)}) copy-start(f32[5,8,8,128]{3,1,2,0:T(8,128)} %copy.76) | copy-start | bytes 491524
  511.2 163.2 %copy-start.9 = (pred[16]{0:T(512)(128)(4,1)S(1)}, pred[16]{0:T(512)(128)(4,1)}, u32[]{:S(2)}) copy-start(pred[16]{0:T(512)(128)(4,1)} %compare_and_fusion.4) | copy-start | bytes 52
  511.2 325.4 %copy-start.1 = (bf16[40,16,640]{2,1,0:T(8,128)(2,1)S(1)}, bf16[40,16,640]{2,1,0:T(8,128)(2,1)}, u32[]{:S(2)}) copy-start(bf16[40,16,640]{2,1,0:T(8,128)(2,1)} %param.16) | copy-start | bytes 2457604
  670.0 14.5 %all-to-all-start = ((f32[4,40,1024]{2,1,0:T(8,128)}), f32[4,40,1024]{2,1,0:T(8,128)}, u32[]{:S(2)}, u32[]{:S(2)}) async-start(f32[4,40,1024]{2,1,0:T(8,128)} %bitcast.113), calls=%async_computation | async-start | bytes 1310720 | tf_op jit(solution)/shard_map/all_to_all | solution.py:91
  674.2 101.9 %all-reduce.3.cloned.1.call-start = ((), (), s32[]{:S(2)}) async-start(), calls=%async_computation.2 | async-start | bytes 327680
  689.0 4.3 collective-permute-start.4
  693.3 4.6 collective-permute-start.5
  697.9 5.7 collective-permute-start.6
  807.8 3.8 collective-permute-start.7
  811.5 3.7 collective-permute-start.8
  815.3 4.6 collective-permute-start.9
  821.7 13.7 %all-to-all-start.1 = ((f32[4,1,40,1024]{3,2,1,0:T(8,128)}), f32[4,1,40,1024]{3,2,1,0:T(8,128)S(1)}, u32[]{:S(2)}, u32[]{:S(2)}) async-start(f32[4,1,40,1024]{3,2,1,0:T(8,128)} %pad_maximum_fusion.1), calls=%async_computation.1 | async-start | bytes 1310720 | tf_op jit(solution)/shard_map/all_to_all | solution.py:145
Sparse Core Ops, SparseCore 0:
  707.3 68.6 all-reduce.2
